TPU v7x, 256 devices: a whole 4x4x8 slice. The times are simulated.
256 devices in a mesh: row: 4 (over y), col: 16 (over x, z_hi), rep: 4 (over z_lo, core).
Axes of the slice: x: 4, y: 4, z: 8 (z_hi: 4, z_lo: 2; z = z_hi * 2 + z_lo), core: 2. Of those that a mesh axis runs over, the one named last changes fastest.
Arguments:
- a_weights: bfloat16 [4, 4096, 2048], P('rep', 'row', 'col'), may hold values from 0 to 10000, as said below
- a_flags: int32 [4, 32, 16], P('rep', 'row', 'col'), may hold values 0 or 1
- b_weights: bfloat16 [4, 2048, 32768], P('rep', 'row', 'col'), may hold values from 0 to 10000, as said below
- b_flags: int32 [4, 16, 256], P('rep', 'row', 'col'), may hold values 0 or 1
- out_flags: int32 [32, 256], P('row', ('col', 'rep')), may hold values 0 or 1
Outputs:
- two_hop: bfloat16 [4096, 32768], P('row', ('col', 'rep'))
Inputs may be any that keep to these rules, and one draw needn't show every extreme that they name: `a_weights`: positive edge weights. `b_weights`: positive edge weights.
All inputs are finite; a program needn't handle non-finite values. No bound on the sum of `a_flags` or of `b_flags` or of `out_flags` on one device may be relied on, other than what follows from the above.
Results may differ from a plain program's by a relative error of at most 0.012.
Values may be sent and summed in bfloat16 or wider, within the bound.
No kernel may reach another device: no remote copies, remote signals or barrier semaphores. Data moves between devices by JAX's collectives and lax.ppermute only.
A program may use at most 64 MiB of HBM per device.

v0:
```python
import jax
import jax.numpy as jnp
from jax import lax
from jax.sharding import PartitionSpec as P


def expand(flags, width):
    return jnp.repeat(jnp.repeat(flags, width, axis=-2), width, axis=-1)


def shards(a_weights, a_flags, b_weights, b_flags, out_flags):
    width = a_weights.shape[1] // a_flags.shape[1]
    a_masked = a_weights * expand(a_flags, width).astype(jnp.bfloat16)
    b_masked = b_weights * expand(b_flags, width).astype(jnp.bfloat16)
    deg_a = 1.0 + lax.psum(jnp.sum(a_masked, axis=(0, 2), dtype=jnp.float32), ("col", "rep"))
    walk_local = (a_masked.astype(jnp.float32) / deg_a[None, :, None]).astype(jnp.bfloat16)
    walk_a = lax.all_gather(walk_local, "col", axis=2, tiled=True)
    deg_b = 1.0 + lax.psum(jnp.sum(b_masked, axis=2, dtype=jnp.float32), "col")
    walk_b = (b_masked.astype(jnp.float32) / deg_b[:, :, None]).astype(jnp.bfloat16)
    left_rows = walk_a[0]
    partial_sum = jnp.dot(
        left_rows,
        lax.all_gather(walk_b, "row", axis=1, tiled=True)[0],
        preferred_element_type=jnp.float32,
    )
    summed = lax.psum_scatter(
        partial_sum.astype(jnp.bfloat16), "rep", scatter_dimension=1, tiled=True
    ).astype(jnp.float32)
    factor = jnp.float32(b_weights.shape[2] * lax.axis_size("col"))
    return (factor * summed * expand(out_flags, width).astype(jnp.float32)).astype(jnp.bfloat16)


def solution(mesh):
    return jax.shard_map(
        shards,
        mesh=mesh,
        in_specs=(
            P("rep", "row", "col"),
            P("rep", "row", "col"),
            P("rep", "row", "col"),
            P("rep", "row", "col"),
            P("row", ("col", "rep")),
        ),
        out_specs=P("row", ("col", "rep")),
        check_vma=False,
    )
```

profile of v0, /device:TPU:1, one launch (start us, length us, event | category | flops | bytes accessed | tf_op | source)
XLA Modules:
  0.0 379.0 jit_solution(2328880365797852931)
XLA Ops:
  6.5 0.7 convert_bitcast_fusion.1
  7.2 0.1 broadcast_bitcast_fusion
  7.3 1.3 convert_reduce_fusion.1
  8.6 128.0 %psum.14 = f32[1024]{0:T(1024)S(1)} all-reduce(f32[1024]{0:T(1024)S(1)} %convert_reduce_fusion.1), channel_id=1, replica_groups=mesh['row'=4,'col'=16,'rep'=4] {'col','rep'}, use_global_device_ids=true, to_apply=%region_1.0 | all-reduce | flops 1024 | bytes 8192 | tf_op jit(solution)/shard_map/psum | solution.py:15
  136.6 2.0 fusion.10
  138.6 0.0 all-gather.3.cloned.1.call-update
  138.6 0.0 all-gather.5.cloned.1.call-start
  138.7 0.7 convert_bitcast_fusion
  139.4 2.3 broadcast_in_dim.20
  141.7 2.8 convert_element_type.80
  144.5 2.2 convert_reduce_fusion
  146.7 33.6 %psum.15 = f32[1,512]{1,0:T(1,128)S(1)} all-reduce(f32[1,512]{1,0:T(1,128)S(1)} %bitcast.29), channel_id=1, replica_groups=mesh['row'=4,'col'=16,'rep'=4] {'col'}, use_global_device_ids=true, to_apply=%region_3.0 | all-reduce | flops 512 | bytes 4096 | tf_op jit(solution)/shard_map/psum | solution.py:18
  180.3 3.9 %fusion.2 = bf16[1,512,2048]{2,1,0:T(8,128)(2,1)} fusion(f32[512]{0:T(512)S(1)} %bitcast.28, bf16[1,512,2048]{2,1,0:T(8,128)(2,1)} %param.7, bf16[1,512,2048]{2,1,0:T(8,128)(2,1)S(1)} %convert_element_type.80), kind=kLoop, calls=%fused_computation.4 | loop fusion | flops 4194304 | bytes 6293504 | tf_op jit(solution)/shard_map/convert_element_type | solution.py:19
  184.2 0.0 all-gather.5.cloned.1.call-update
  184.2 0.0 reduce-scatter.2.cloned.1.call-start
  184.3 36.4 %all-gather.3.cloned.1.call-done = bf16[1,1024,2048]{2,1,0:T(8,128)(2,1)} async-done(((bf16[1,1024,128]{2,1,0:T(8,128)(2,1)}), bf16[1,1024,2048]{2,1,0:T(8,128)(2,1)}) %all-gather.3.cloned.1.call-update) | async-done | bytes 4194320 | tf_op jit(solution)/shard_map/all_gather | solution.py:17
  220.6 86.0 %all-gather.5.cloned.1.call-done = bf16[1,2048,2048]{2,1,0:T(8,128)(2,1)} async-done(((bf16[1,512,2048]{2,1,0:T(8,128)(2,1)}), bf16[1,2048,2048]{2,1,0:T(8,128)(2,1)}) %all-gather.5.cloned.1.call-update) | async-done | bytes 8388624 | tf_op jit(solution)/shard_map/all_gather | solution.py:23
  306.6 13.8 %fusion.4 = bf16[1024,2048]{1,0:T(8,128)(2,1)} fusion(bf16[1,2048,2048]{2,1,0:T(8,128)(2,1)} %all-gather.5.cloned.1.call-done, bf16[1,1024,2048]{2,1,0:T(8,128)(2,1)} %all-gather.3.cloned.1.call-done), kind=kOutput, calls=%fused_computation.6 | convolution fusion | flops 8592031744 | bytes 16777216 | tf_op jit(solution)/shard_map/dot_general | solution.py:21
  320.4 0.0 reduce-scatter.2.cloned.1.call-update
  320.4 0.7 copy-done.1
  321.1 0.1 copy.6
  321.2 48.7 %reduce-scatter.2.cloned.1.call-done = bf16[1024,512]{1,0:T(8,128)(2,1)} async-done(((bf16[1024,2048]{1,0:T(8,128)(2,1)}), bf16[1024,512]{1,0:T(8,128)(2,1)}) %reduce-scatter.2.cloned.1.call-update) | async-done | bytes 1048592 | tf_op jit(solution)/shard_map/reduce_scatter | solution.py:26
  369.9 1.2 broadcast_in_dim.22
  371.1 1.4 fusion.9
  (9 shorter events, 0.1 us)
Async XLA Ops:
  6.5 214.1 %all-gather.3.cloned.1.call-start = ((), (), s32[]{:S(2)}) async-start(), calls=%async_computation.1 | async-start | bytes 4456448 | tf_op jit(solution)/shard_map/all_gather | solution.py:17
  138.6 168.0 %all-gather.5.cloned.1.call-start = ((), (), s32[]{:S(2)}) async-start(), calls=%async_computation.2 | async-start | bytes 10485760 | tf_op jit(solution)/shard_map/all_gather | solution.py:23
  184.2 185.6 %reduce-scatter.2.cloned.1.call-start = ((), (), s32[]{:S(2)}) async-start(), calls=%async_computation.3 | async-start | bytes 5242880 | tf_op jit(solution)/shard_map/reduce_scatter | solution.py:26
  320.4 0.7 copy-start.1
  369.8 1.3 copy-start
Sparse Core Ops, SparseCore 0:
  138.7 81.8 all-gather.2
  222.4 84.1 all-gather.4
  320.6 49.2 reduce-scatter.1
where the time goes:
time: 379 us
  waiting for transfers between devices  171 us (45%)
  blocking collectives  162 us (43%)
  matrix products  13.8 us (4%)
  between operations  13.1 us (3%)
  other arithmetic  12.1 us (3%)
  local copies, waits for them, and re-layouts  7.21 us (2%)
    psum x1, blocking collectives, shards(): lax.psum(jnp.sum(a_masked, axis=(0, 2), dtype=jnp.float32), ('col', 'rep'))  128 us
    all_gather x1, waiting for transfers between devices, shards(): lax.all_gather(walk_b, 'row', axis=1, tiled=True)[0]  86 us
    reduce_scatter x1, waiting for transfers between devices, shards(): lax.psum_scatter(partial_sum.astype(jnp.bfloat16), 'rep', scatter_dimensi...  48.7 us
    all_gather x1, waiting for transfers between devices, shards(): walk_a = lax.all_gather(walk_local, 'col', axis=2, tiled=True)  36.4 us
    psum x1, blocking collectives, shards(): deg_b = 1.0 + lax.psum(jnp.sum(b_masked, axis=2, dtype=jnp.float32), 'col')  33.6 us
    dot_general x1, matrix products, shards(): jnp.dot(left_rows, lax.all_gather(walk_b, 'row', axis=1, tiled=True)[0],...  13.8 us
  transfers between devices with their start and end apart: 3, of which 3 were waited for; matrix products, arithmetic and copies ran while one was open for 3% of the time, Pallas kernels for 0%

commit v1 on v0

--- a/solution.py
+++ b/solution.py
@@ -12,7 +12,9 @@
     width = a_weights.shape[1] // a_flags.shape[1]
     a_masked = a_weights * expand(a_flags, width).astype(jnp.bfloat16)
     b_masked = b_weights * expand(b_flags, width).astype(jnp.bfloat16)
-    deg_a = 1.0 + lax.psum(jnp.sum(a_masked, axis=(0, 2), dtype=jnp.float32), ("col", "rep"))
+    deg_a = 1.0 + lax.psum(
+        lax.psum(jnp.sum(a_masked, axis=(0, 2), dtype=jnp.float32), "rep"), "col"
+    )
     walk_local = (a_masked.astype(jnp.float32) / deg_a[None, :, None]).astype(jnp.bfloat16)
     walk_a = lax.all_gather(walk_local, "col", axis=2, tiled=True)
     deg_b = 1.0 + lax.psum(jnp.sum(b_masked, axis=2, dtype=jnp.float32), "col")

time: 379 us -> 307 us (0.81)
  blocking collectives: 162 us -> 47.4 us
  waiting for transfers between devices: 171 us -> 216 us
    psum x1, blocking collectives: 128 us -> 8.26 us  [shards(): lax.psum(jnp.sum(a_masked, axis=(0, 2), dtype=jnp.float32), 'rep')]
    all_gather x1, waiting for transfers between devices: 36.4 us -> 81.2 us  [shards(): walk_a = lax.all_gather(walk_local, 'col', axis=2, tiled=True)]
    psum x1, blocking collectives: 33.6 us -> 39.2 us  [shards(): deg_b = 1.0 + lax.psum(jnp.sum(b_masked, axis=2, dtype=jnp.float32), 'col')]
  transfers between devices with their start and end apart: 3 -> 3, of which waited for: 3 -> 3; matrix products, arithmetic and copies ran while one was open for 3% -> 1% of each run, Pallas kernels for 0% -> 0%
where the time goes in v1:
time: 307 us
  waiting for transfers between devices  216 us (70%)
  blocking collectives  47.4 us (15%)
  matrix products  13.8 us (4%)
  between operations  13.2 us (4%)
  other arithmetic  9.59 us (3%)
  local copies, waits for them, and re-layouts  7.25 us (2%)
    all_gather x1, waiting for transfers between devices, shards(): lax.all_gather(walk_b, 'row', axis=1, tiled=True)[0]  85.8 us
    all_gather x1, waiting for transfers between devices, shards(): walk_a = lax.all_gather(walk_local, 'col', axis=2, tiled=True)  81.2 us
    reduce_scatter x1, waiting for transfers between devices, shards(): lax.psum_scatter(partial_sum.astype(jnp.bfloat16), 'rep', scatter_dimensi...  48.7 us
    psum x1, blocking collectives, shards(): deg_b = 1.0 + lax.psum(jnp.sum(b_masked, axis=2, dtype=jnp.float32), 'col')  39.2 us
    dot_general x1, matrix products, shards(): jnp.dot(left_rows, lax.all_gather(walk_b, 'row', axis=1, tiled=True)[0],...  13.8 us
    psum x1, blocking collectives, shards(): lax.psum(jnp.sum(a_masked, axis=(0, 2), dtype=jnp.float32), 'rep')  8.26 us
  transfers between devices with their start and end apart: 3, of which 3 were waited for; matrix products, arithmetic and copies ran while one was open for 1% of the time, Pallas kernels for 0%

profile of v1, /device:TPU:1, one launch (start us, length us, event | category | flops | bytes accessed | tf_op | source)
XLA Modules:
  0.0 307.1 jit_solution(14390262425811864992)
XLA Ops:
  6.5 0.7 convert_bitcast_fusion
  7.2 2.3 broadcast_in_dim.20
  9.5 2.9 convert_element_type.80
  12.4 0.0 copy-done.3
  12.4 0.1 broadcast_bitcast_fusion
  12.5 0.4 convert_reduce_fusion.1
  12.9 8.3 %psum.21 = f32[1024]{0:T(1024)S(1)} all-reduce(f32[1024]{0:T(1024)S(1)} %convert_reduce_fusion.1), channel_id=1, replica_groups=mesh['row'=4,'col'=16,'rep'=4] {'rep'}, use_global_device_ids=true, to_apply=%region_1.0 | all-reduce | flops 1024 | bytes 8192 | tf_op jit(solution)/shard_map/psum | solution.py:16
  21.1 2.2 convert_reduce_fusion
  23.3 39.2 %all-reduce = (f32[1,512]{1,0:T(1,128)S(1)}, f32[1024]{0:T(1024)S(1)}) all-reduce(f32[1,512]{1,0:T(1,128)S(1)} %bitcast.28, f32[1024]{0:T(1024)S(1)} %psum.21), channel_id=1, replica_groups=mesh['row'=4,'col'=16,'rep'=4] {'col'}, use_global_device_ids=true, to_apply=%region_4.0 | all-reduce | flops 1536 | bytes 12288 | tf_op jit(solution)/shard_map/psum | solution.py:20
  62.5 1.0 fusion.10
  63.6 0.0 all-gather.3.cloned.1.call-update
  63.6 0.0 all-gather.5.cloned.1.call-start
  63.7 3.9 %fusion.2 = bf16[1,512,2048]{2,1,0:T(8,128)(2,1)} fusion(f32[512]{0:T(512)S(1)} %bitcast.29, bf16[1,512,2048]{2,1,0:T(8,128)(2,1)} %param.7, bf16[1,512,2048]{2,1,0:T(8,128)(2,1)S(1)} %convert_element_type.80), kind=kLoop, calls=%fused_computation.4 | loop fusion | flops 4194304 | bytes 6293504 | tf_op jit(solution)/shard_map/convert_element_type | solution.py:21
  67.5 0.0 all-gather.5.cloned.1.call-update
  67.6 0.0 reduce-scatter.2.cloned.1.call-start
  67.6 81.2 %all-gather.3.cloned.1.call-done = bf16[1,1024,2048]{2,1,0:T(8,128)(2,1)} async-done(((bf16[1,1024,128]{2,1,0:T(8,128)(2,1)}), bf16[1,1024,2048]{2,1,0:T(8,128)(2,1)}) %all-gather.3.cloned.1.call-update) | async-done | bytes 4194320 | tf_op jit(solution)/shard_map/all_gather | solution.py:19
  148.8 85.8 %all-gather.5.cloned.1.call-done = bf16[1,2048,2048]{2,1,0:T(8,128)(2,1)} async-done(((bf16[1,512,2048]{2,1,0:T(8,128)(2,1)}), bf16[1,2048,2048]{2,1,0:T(8,128)(2,1)}) %all-gather.5.cloned.1.call-update) | async-done | bytes 8388624 | tf_op jit(solution)/shard_map/all_gather | solution.py:25
  234.6 13.8 %fusion.4 = bf16[1024,2048]{1,0:T(8,128)(2,1)} fusion(bf16[1,2048,2048]{2,1,0:T(8,128)(2,1)} %all-gather.5.cloned.1.call-done, bf16[1,1024,2048]{2,1,0:T(8,128)(2,1)} %all-gather.3.cloned.1.call-done), kind=kOutput, calls=%fused_computation.6 | convolution fusion | flops 8592031744 | bytes 16777216 | tf_op jit(solution)/shard_map/dot_general | solution.py:23
  248.4 0.0 reduce-scatter.2.cloned.1.call-update
  248.5 0.7 copy-done.2
  249.1 0.1 copy.6
  249.2 48.7 %reduce-scatter.2.cloned.1.call-done = bf16[1024,512]{1,0:T(8,128)(2,1)} async-done(((bf16[1024,2048]{1,0:T(8,128)(2,1)}), bf16[1024,512]{1,0:T(8,128)(2,1)}) %reduce-scatter.2.cloned.1.call-update) | async-done | bytes 1048592 | tf_op jit(solution)/shard_map/reduce_scatter | solution.py:28
  297.9 1.2 broadcast_in_dim.22
  299.2 1.4 fusion.9
  (13 shorter events, 0.1 us)
Async XLA Ops:
  6.5 142.3 %all-gather.3.cloned.1.call-start = ((), (), s32[]{:S(2)}) async-start(), calls=%async_computation.1 | async-start | bytes 4456448 | tf_op jit(solution)/shard_map/all_gather | solution.py:19
  9.5 2.9 copy-start.3
  9.5 3.0 copy-start
  63.6 171.0 %all-gather.5.cloned.1.call-start = ((), (), s32[]{:S(2)}) async-start(), calls=%async_computation.2 | async-start | bytes 10485760 | tf_op jit(solution)/shard_map/all_gather | solution.py:25
  67.6 230.3 %reduce-scatter.2.cloned.1.call-start = ((), (), s32[]{:S(2)}) async-start(), calls=%async_computation.3 | async-start | bytes 5242880 | tf_op jit(solution)/shard_map/reduce_scatter | solution.py:28
  248.4 0.7 copy-start.2
  297.9 1.3 copy-start.1
Sparse Core Ops, SparseCore 0:
  63.7 85.0 all-gather.2
  150.6 83.9 all-gather.4
  248.6 49.2 reduce-scatter.1

commit v2 on v0

--- a/solution.py
+++ b/solution.py
@@ -20,7 +20,9 @@
     left_rows = walk_a[0]
     partial_sum = jnp.dot(
         left_rows,
-        lax.all_gather(walk_b, "row", axis=1, tiled=True)[0],
+        jnp.concatenate(
+            lax.all_to_all(jnp.stack([walk_b] * lax.axis_size("row")), "row", 0, 0), axis=1
+        )[0],
         preferred_element_type=jnp.float32,
     )
     summed = lax.psum_scatter(

time: 379 us -> 350 us (0.923)
  waiting for transfers between devices: 171 us -> 57 us
  blocking collectives: 162 us -> 246 us
    all_gather x1 -> x0, waiting for transfers between devices: 86 us -> none  [shards(): lax.all_gather(walk_b, 'row', axis=1, tiled=True)[0]]
    all_to_all x0 -> x1, blocking collectives: none -> 84.7 us  [shards(): lax.all_to_all(jnp.stack([walk_b] * lax.axis_size('row')), 'row', 0, 0)]
    all_gather x1, waiting for transfers between devices: 36.4 us -> 0.01 us  [shards(): walk_a = lax.all_gather(walk_local, 'col', axis=2, tiled=True)]
    reduce_scatter x1, waiting for transfers between devices: 48.7 us -> 56.9 us  [shards(): lax.psum_scatter(partial_sum.astype(jnp.bfloat16), 'rep', scatter_dimensi...]
  transfers between devices with their start and end apart: 3 -> 2, of which waited for: 3 -> 1; matrix products, arithmetic and copies ran while one was open for 3% -> 3% of each run, Pallas kernels for 0% -> 0%
where the time goes in v2:
time: 350 us
  blocking collectives  246 us (70%)
  waiting for transfers between devices  57 us (16%)
  matrix products  13.8 us (4%)
  between operations  13.5 us (4%)
  other arithmetic  10.8 us (3%)
  local copies, waits for them, and re-layouts  8.29 us (2%)
    psum x1, blocking collectives, shards(): lax.psum(jnp.sum(a_masked, axis=(0, 2), dtype=jnp.float32), ('col', 'rep'))  128 us
    all_to_all x1, blocking collectives, shards(): lax.all_to_all(jnp.stack([walk_b] * lax.axis_size('row')), 'row', 0, 0)  84.7 us
    reduce_scatter x1, waiting for transfers between devices, shards(): lax.psum_scatter(partial_sum.astype(jnp.bfloat16), 'rep', scatter_dimensi...  56.9 us
    psum x1, blocking collectives, shards(): deg_b = 1.0 + lax.psum(jnp.sum(b_masked, axis=2, dtype=jnp.float32), 'col')  33.6 us
    dot_general x1, matrix products, shards(): jnp.dot(left_rows, jnp.concatenate(lax.all_to_all(jnp.stack([walk_b] * la...  13.8 us
  transfers between devices with their start and end apart: 2, of which 1 were waited for; matrix products, arithmetic and copies ran while one was open for 3% of the time, Pallas kernels for 0%

profile of v2, /device:TPU:1, one launch (start us, length us, event | category | flops | bytes accessed | tf_op | source)
XLA Modules:
  0.0 349.7 jit_solution(8260688940077643840)
XLA Ops:
  6.5 0.0 all-gather.2.cloned.1.call-start
  6.5 0.7 convert_bitcast_fusion.1
  7.2 0.1 broadcast_bitcast_fusion
  7.3 1.3 convert_reduce_fusion.1
  8.6 128.0 %psum.14 = f32[1024]{0:T(1024)S(1)} all-reduce(f32[1024]{0:T(1024)S(1)} %convert_reduce_fusion.1), channel_id=1, replica_groups=mesh['row'=4,'col'=16,'rep'=4] {'col','rep'}, use_global_device_ids=true, to_apply=%region_1.0 | all-reduce | flops 1024 | bytes 8192 | tf_op jit(solution)/shard_map/psum | solution.py:15
  136.6 2.0 fusion.8
  138.6 0.0 all-gather.2.cloned.1.call-update
  138.6 0.0 reduce-scatter.2.cloned.1.call-start
  138.7 0.7 convert_bitcast_fusion
  139.4 2.3 broadcast_in_dim.20
  141.7 2.8 convert_element_type.82
  144.5 2.2 convert_reduce_fusion
  146.7 33.6 %psum.15 = f32[1,512]{1,0:T(1,128)S(1)} all-reduce(f32[1,512]{1,0:T(1,128)S(1)} %bitcast.29), channel_id=1, replica_groups=mesh['row'=4,'col'=16,'rep'=4] {'col'}, use_global_device_ids=true, to_apply=%region_3.0 | all-reduce | flops 512 | bytes 4096 | tf_op jit(solution)/shard_map/psum | solution.py:18
  180.3 2.5 fusion.6
  182.8 1.1 stack.2
  183.9 84.7 %all_to_all.5 = bf16[4,1,512,2048]{3,2,1,0:T(8,128)(2,1)} all-to-all(bf16[4,1,512,2048]{3,2,1,0:T(8,128)(2,1)S(1)} %stack.2), channel_id=1, replica_groups=mesh['row'=4,'col'=16,'rep'=4] {'row'}, dimensions={0} | all-to-all | bytes 16777216 | tf_op jit(solution)/shard_map/all_to_all | solution.py:24
  268.6 13.8 %fusion.3 = bf16[1024,2048]{1,0:T(8,128)(2,1)} fusion(bf16[2048,2048]{1,0:T(8,128)(2,1)} %bitcast.25, bf16[1,1024,2048]{2,1,0:T(8,128)(2,1)} %all-gather.2.cloned.1.call-done), kind=kOutput, calls=%fused_computation.5 | convolution fusion | flops 8592031744 | bytes 16777216 | tf_op jit(solution)/shard_map/dot_general | solution.py:21
  282.5 0.0 reduce-scatter.2.cloned.1.call-update
  282.5 0.7 copy-done.1
  283.1 0.1 copy.6
  283.2 56.9 %reduce-scatter.2.cloned.1.call-done = bf16[1024,512]{1,0:T(8,128)(2,1)} async-done(((bf16[1024,2048]{1,0:T(8,128)(2,1)}), bf16[1024,512]{1,0:T(8,128)(2,1)}) %reduce-scatter.2.cloned.1.call-update) | async-done | bytes 1048592 | tf_op jit(solution)/shard_map/reduce_scatter | solution.py:28
  340.2 1.2 broadcast_in_dim.22
  341.4 0.0 copy-done
  341.5 1.4 fusion.7
  (8 shorter events, 0.1 us)
Async XLA Ops:
  6.5 262.1 %all-gather.2.cloned.1.call-start = ((), (), s32[]{:S(2)}) async-start(), calls=%async_computation.2 | async-start | bytes 4456448 | tf_op jit(solution)/shard_map/all_gather | solution.py:17
  138.6 201.5 %reduce-scatter.2.cloned.1.call-start = ((), (), s32[]{:S(2)}) async-start(), calls=%async_computation.3 | async-start | bytes 5242880 | tf_op jit(solution)/shard_map/reduce_scatter | solution.py:28
  282.4 0.7 copy-start.1
  340.2 1.3 copy-start
Sparse Core Ops, SparseCore 0:
  138.7 81.8 all-gather.1
  282.6 57.5 reduce-scatter.1
